TPU v7x, 256 devices: a whole 4x4x8 slice. The times are simulated.
256 devices in a mesh: gx: 16 (over x_hi, z), gz: 16 (over x_lo, y, core).
Axes of the slice: x: 4 (x_hi: 2, x_lo: 2; x = x_hi * 2 + x_lo), y: 4, z: 8, core: 2. Of those that a mesh axis runs over, the one named last changes fastest.
Arguments:
- direct_modes: bfloat16 [3, 256, 1024, 128], P(None, 'gx', 'gz'), may hold values from -6 to 6
- adjoint_modes: bfloat16 [3, 256, 1024, 128], P(None, 'gx', 'gz'), may hold values from -0.0048828125 to 0.0048828125
- stencil_taps: float32 [36, 256, 1024], P(None, 'gx', 'gz'), may hold values from -0.72 to 0.72
- coupling: float32 [18, 256, 1024], P(None, 'gx', 'gz'), may hold values from -1.2 to 1.2
Outputs:
- evolved: bfloat16 [3, 256, 1024, 128], P(None, 'gx', 'gz')
- reduced: float32 [64, 64], P('gx')
All inputs are finite; a program needn't handle non-finite values.
Results may differ from a plain program's by a relative error of at most 0.0031.
Values sent between devices are 32-bit elements; how exact they have to be, the bound alone decides.
A program may use at most 64 MiB of HBM per device.

v0:
```python
import jax
import jax.numpy as jnp
from jax import lax
from jax.sharding import PartitionSpec as P

STEPS = 4


def with_halo(x, sides, width):
    for axis, dim in sides:
        peers, length = (lax.axis_size(axis), x.shape[dim])
        up = [(i, (i + 1) % peers) for i in range(peers)]
        down = [(j, i) for i, j in up]
        last = lax.slice_in_dim(x, length - width, length, axis=dim)
        leading = lax.slice_in_dim(x, 0, width, axis=dim)
        before = lax.ppermute(last, axis, up)
        after = lax.ppermute(leading, axis, down)
        x = jnp.concatenate([before, x, after], axis=dim)
    return x


def lane_weight(lower, first, second):
    return jnp.where(lower, first[:, :, None], second[:, :, None])


def advance(padded, tap_block, mix_block):
    width_x = padded.shape[1] - 2
    width_z = padded.shape[2] - 2
    lanes_all = padded.shape[3]
    half = lanes_all // 2
    lower = lax.broadcasted_iota(jnp.int32, (1, 1, lanes_all), 2) < half
    swapped = jnp.concatenate((padded[:, :, :, half:], padded[:, :, :, :half]), axis=3)
    own = padded[:, 1 : 1 + width_x, 1 : 1 + width_z, :]
    total = jnp.zeros((3, width_x, width_z, lanes_all), jnp.float32)
    for side_at in range(2):
        source = padded if side_at == 0 else swapped
        for tap_at in range(9):
            shift_x = tap_at // 3
            shift_z = tap_at % 3
            shifted = source[:, shift_x : shift_x + width_x, shift_z : shift_z + width_z, :]
            weight = lane_weight(
                lower, tap_block[side_at * 9 + tap_at], tap_block[18 + side_at * 9 + tap_at]
            )
            total = total + weight[None] * shifted
    mixed = []
    for comp_at in range(3):
        term = jnp.zeros((width_x, width_z, lanes_all), jnp.float32)
        for other_at in range(3):
            weight = lane_weight(
                lower, mix_block[comp_at * 3 + other_at], mix_block[9 + comp_at * 3 + other_at]
            )
            term = term + weight * own[other_at]
        mixed.append(term)
    return own + total + jnp.stack(mixed, axis=0)


def plane_product(adjoint_flat, evolved_flat):
    result = jnp.zeros((adjoint_flat.shape[2], evolved_flat.shape[2]), jnp.float32)
    for plane_at in range(2):
        result = result + lax.dot_general(
            adjoint_flat[:, plane_at, :],
            evolved_flat[:, plane_at, :],
            (((0,), (0,)), ((), ())),
            preferred_element_type=jnp.float32,
        )
    return result


def body(direct_modes, adjoint_modes, stencil_taps, coupling):
    state = direct_modes.astype(jnp.float32)
    modes = state.shape[3] // 2
    for step in range(STEPS):
        padded = with_halo(state, (("gx", 1), ("gz", 2)), 1)
        state = advance(padded, stencil_taps, coupling)
    evolved = state.astype(jnp.bfloat16)
    adjoint_flat = adjoint_modes.reshape(-1, 2, modes)
    evolved_flat = evolved.reshape(-1, 2, modes)
    partial_sum = plane_product(adjoint_flat, evolved_flat)
    spanned = lax.psum(partial_sum, "gz")
    reduced = lax.psum_scatter(spanned, "gx", scatter_dimension=0, tiled=True)
    return (evolved, reduced)


def solution(mesh):
    placed = (
        P(None, "gx", "gz", None),
        P(None, "gx", "gz", None),
        P(None, "gx", "gz"),
        P(None, "gx", "gz"),
    )
    return jax.shard_map(
        body,
        mesh=mesh,
        in_specs=placed,
        out_specs=(P(None, "gx", "gz", None), P("gx", None)),
        check_vma=False,
    )
```

profile of v0, /device:TPU:2, one launch (start us, length us, event | category | flops | bytes accessed | tf_op | source)
XLA Modules:
  0.0 267.7 jit_solution(13567518144057242414)
XLA Ops:
  0.6 1.6 fusion.176
  2.2 7.4 %collective-permute-start.1 = (f32[3,1,64,128]{3,2,1,0:T(8,128)}, f32[3,1,64,128]{3,2,1,0:T(8,128)S(1)}, u32[]{:S(2)}, u32[]{:S(2)}) collective-permute-start(f32[3,1,64,128]{3,2,1,0:T(8,128)} %get-tuple-element.51), channel_id=1, source_target_pairs={{16,0},{32,16},{48,32},{64,48},{80,64},{96,80},{112,96},{128,112},... | collective-permute-start | bytes 294920 | tf_op jit(solution)/shard_map/ppermute | solution.py:17
  9.6 1.3 convert_element_type.6
  10.9 0.7 slice_bitcast_fusion.53
  11.6 0.7 slice_bitcast_fusion.52
  12.3 3.2 %reshape.117 = bf16[3072,2,64]{2,1,0:T(2,128)(2,1)S(1)} reshape(bf16[3,16,64,128]{3,2,1,0:T(8,128)(2,1)} %param.5) | data formatting | bytes 1572864 | tf_op jit(solution)/shard_map/reshape | solution.py:76
  15.7 3.5 %fusion.172 = (bf16[3072,1,64]{2,1,0:T(2,128)(2,1)}, bf16[3072,1,64]{2,1,0:T(2,128)(2,1)}) fusion(bf16[3072,2,64]{2,1,0:T(2,128)(2,1)S(1)} %reshape.117), kind=kLoop, calls=%fused_computation.399 | loop fusion | bytes 1572864 | tf_op jit(solution)/shard_map/slice | solution.py:61
  19.5 3.9 %broadcast_select_fusion.8 = (f32[16,64,128]{2,1,0:T(8,128)S(1)}, f32[16,64,128]{2,1,0:T(8,128)S(1)}, f32[16,64,128]{2,1,0:T(8,128)S(1)}, f32[16,64,128]{2,1,0:T...) fusion(f32[16,64]{1,0:T(8,128)S(1)} %copy-done.47, ...), kind=kLoop, calls=%fused_computation.316 | loop fusion | flops 1179648 | bytes 4792448 | tf_op jit(solution)/shard_map/jit(_where)/select_n | solution.py:23
  23.4 4.1 %broadcast_select_fusion.17 = (f32[16,64,128]{2,1,0:T(8,128)}, f32[16,64,128]{2,1,0:T(8,128)}, f32[16,64,128]{2,1,0:T(8,128)}, f32[16,64,128]{2,1,0:T(8,128)}, f...) fusion(f32[16,64]{1,0:T(8,128)S(1)} %get-tuple-element.71, ...), kind=kLoop, calls=%fused_computation.325 | loop fusion | flops 1179648 | bytes 4792448 | tf_op jit(solution)/shard_map/jit(_where)/select_n | solution.py:23
  27.6 2.9 %fusion.139 = (f32[1,16,64,128]{3,2,1,0:T(8,128)}, f32[1,16,64,128]{3,2,1,0:T(8,128)}) fusion(f32[3,16,64,128]{3,2,1,0:T(8,128)S(1)} %convert_element_type.6, f32[16,64]{1,0:T(8,128)S(1)} %get-tuple-element.99, f32[16,64]{1,0:T(8,128)S(1)} %get-tuple-element.100, f32[16,64]{1,0:T(8,128)S(1)} %get-tuple-element.101, f32[16,64]{1,0:T(8,128)S(1)} %get-tuple-element.102, ...), kind=kLoop, calls=%fused_computation.280 | loop fusion | flops 2097152 | bytes 2670720 | tf_op jit(solution)/shard_map/add | solution.py:52
  30.4 0.7 pad_maximum_fusion.31
  31.1 3.0 %collective-permute-start.3 = (f32[3,18,1,128]{3,2,1,0:T(1,128)}, f32[3,18,1,128]{3,2,1,0:T(1,128)S(1)}, u32[]{:S(2)}, u32[]{:S(2)}) collective-permute-start(f32[3,18,1,128]{3,2,1,0:T(1,128)} %get-tuple-element.31), channel_id=1, source_target_pairs={{1,0},{2,1},{3,2},{4,3},{5,4},{6,5},{7,6},{8,7},{9,8},{10,9},{11,1... | collective-permute-start | bytes 82952 | tf_op jit(solution)/shard_map/ppermute | solution.py:17
  34.1 1.7 fusion.155
  35.8 4.1 %copy.18 = bf16[3072,1,64]{0,2,1:T(8,128)(2,1)} copy(bf16[3072,1,64]{2,1,0:T(2,128)(2,1)} %get-tuple-element.43) | data formatting | bytes 786432
  39.9 4.1 %copy.20 = bf16[3072,1,64]{0,2,1:T(8,128)(2,1)} copy(bf16[3072,1,64]{2,1,0:T(2,128)(2,1)} %get-tuple-element.42) | data formatting | bytes 786432
  44.0 0.6 dynamic-slice
  45.3 0.3 pad_maximum_fusion.1
  45.6 0.6 fusion.170
  46.4 0.4 maximum_maximum_fusion
  47.5 0.3 copy-done
  49.4 6.4 %fusion.106 = f32[3,16,64,128]{3,2,1,0:T(8,128)S(1)} fusion(f32[3,16,64,128]{3,2,1,0:T(8,128)S(1)} %convert_element_type.6, f32[3,18,66,64]{3,2,1,0:T(8,128)S(1)} %get-tuple-element.15, f32[3,18,66,64]{3,2,1,0:T(8,128)S(1)} %get-tuple-element.14, f32[3,18,65,128]{3,2,1,0:T(8,128)S(1)} %get-tuple-element.29, ...), kind=kLoop, calls=%fused_computation.188 | loop fusion | flops 19660800 | bytes 25614336 | tf_op jit(solution)/shard_map/add | solution.py:54
  55.9 5.0 %collective-permute-start.5 = (f32[3,1,64,128]{3,2,1,0:T(8,128)S(1)}, f32[3,1,64,128]{3,2,1,0:T(8,128)S(1)}, u32[]{:S(2)}, u32[]{:S(2)}) collective-permute-start(f32[3,1,64,128]{3,2,1,0:T(8,128)S(1)} %get-tuple-element.49), channel_id=1, source_target_pairs={{16,0},{32,16},{48,32},{64,48},{80,64},{96,80},{112,96},{128,112},... | collective-permute-start | bytes 294920 | tf_op jit(solution)/shard_map/ppermute | solution.py:17
  60.9 2.0 fusion.141
  62.8 0.3 collective-permute-done.5
  63.1 6.0 %collective-permute-done.4 = f32[3,1,64,128]{3,2,1,0:T(8,128)S(1)} collective-permute-done((f32[3,1,64,128]{3,2,1,0:T(8,128)S(1)}, f32[3,1,64,128]{3,2,1,0:T(8,128)S(1)}, u32[]{:S(2)}, u32[]{:S(2)}) %collective-permute-start.4) | collective-permute-done | bytes 98336 | tf_op jit(solution)/shard_map/ppermute | solution.py:16
  69.1 3.1 %collective-permute-start.7 = (f32[3,18,1,128]{3,2,1,0:T(1,128)S(1)}, f32[3,18,1,128]{3,2,1,0:T(1,128)S(1)}, u32[]{:S(2)}, u32[]{:S(2)}) collective-permute-start(f32[3,18,1,128]{3,2,1,0:T(1,128)S(1)} %get-tuple-element.27), channel_id=1, source_target_pairs={{1,0},{2,1},{3,2},{4,3},{5,4},{6,5},{7,6},{8,7},{9,8},{10,9},{11,1... | collective-permute-start | bytes 82952 | tf_op jit(solution)/shard_map/ppermute | solution.py:17
  72.2 1.0 fusion.157
  73.2 0.6 collective-permute-done.7
  73.8 3.8 %collective-permute-done.6 = f32[3,18,1,128]{3,2,1,0:T(1,128)S(1)} collective-permute-done((f32[3,18,1,128]{3,2,1,0:T(1,128)S(1)}, f32[3,18,1,128]{3,2,1,0:T(1,128)S(1)}, u32[]{:S(2)}, u32[]{:S(2)}) %collective-permute-start.6) | collective-permute-done | bytes 27680 | tf_op jit(solution)/shard_map/ppermute | solution.py:16
  77.6 0.3 pad_maximum_fusion.3
  77.9 0.6 fusion.169
  78.6 0.4 maximum_maximum_fusion.1
  78.9 6.5 %fusion.72 = f32[3,16,64,128]{3,2,1,0:T(8,128)S(1)} fusion(f32[3,16,64,128]{3,2,1,0:T(8,128)S(1)} %fusion.106, f32[3,18,66,64]{3,2,1,0:T(8,128)S(1)} %get-tuple-element.13, f32[3,18,66,64]{3,2,1,0:T(8,128)S(1)} %get-tuple-element.12, f32[3,18,65,128]{3,2,1,0:T(8,128)S(1)} %get-tuple-element.25, f32[3,1,64,128]{3,2,1,0:T(8,128)S(1)} %collective-permute-done.5, ...), kind=kLoop, calls=%fused_computation.131 | loop fusion | flops 19660800 | bytes 25614336 | tf_op jit(solution)/shard_map/add | solution.py:54
  85.5 2.0 collective-permute-start.8
  87.5 2.0 fusion.143
  89.5 0.6 collective-permute-done.9
  90.1 3.7 %collective-permute-done.8 = f32[3,1,64,128]{3,2,1,0:T(8,128)S(1)} collective-permute-done((f32[3,1,64,128]{3,2,1,0:T(8,128)S(1)}, f32[3,1,64,128]{3,2,1,0:T(8,128)S(1)}, u32[]{:S(2)}, u32[]{:S(2)}) %collective-permute-start.8) | collective-permute-done | bytes 98336 | tf_op jit(solution)/shard_map/ppermute | solution.py:16
  94.0 0.5 collective-permute-start.10
  94.5 1.0 fusion.159
  95.5 4.1 %collective-permute-done.10 = f32[3,18,1,128]{3,2,1,0:T(1,128)S(1)} collective-permute-done((f32[3,18,1,128]{3,2,1,0:T(1,128)S(1)}, f32[3,18,1,128]{3,2,1,0:T(1,128)S(1)}, u32[]{:S(2)}, u32[]{:S(2)}) %collective-permute-start.10) | collective-permute-done | bytes 27680 | tf_op jit(solution)/shard_map/ppermute | solution.py:16
  99.7 0.3 pad_maximum_fusion.5
  99.9 0.6 fusion.168
  100.6 0.4 maximum_maximum_fusion.2
  101.0 6.5 %fusion.38 = f32[3,16,64,128]{3,2,1,0:T(8,128)S(1)} fusion(f32[3,16,64,128]{3,2,1,0:T(8,128)S(1)} %fusion.72, f32[3,18,66,64]{3,2,1,0:T(8,128)S(1)} %get-tuple-element.11, f32[3,18,66,64]{3,2,1,0:T(8,128)S(1)} %get-tuple-element.10, f32[3,18,65,128]{3,2,1,0:T(8,128)S(1)} %get-tuple-element.21, f32[3,1,64,128]{3,2,1,0:T(8,128)S(1)} %collective-permute-done.9, ...), kind=kLoop, calls=%fused_computation.74 | loop fusion | flops 19660800 | bytes 25614336 | tf_op jit(solution)/shard_map/add | solution.py:54
  107.6 2.0 collective-permute-start.12
  109.6 2.0 fusion.145
  111.5 0.6 collective-permute-done.13
  112.2 3.7 %collective-permute-done.12 = f32[3,1,64,128]{3,2,1,0:T(8,128)S(1)} collective-permute-done((f32[3,1,64,128]{3,2,1,0:T(8,128)S(1)}, f32[3,1,64,128]{3,2,1,0:T(8,128)S(1)}, u32[]{:S(2)}, u32[]{:S(2)}) %collective-permute-start.12) | collective-permute-done | bytes 98336 | tf_op jit(solution)/shard_map/ppermute | solution.py:16
  116.0 0.5 collective-permute-start.14
  116.5 1.0 fusion.161
  117.5 4.2 %collective-permute-done.14 = f32[3,18,1,128]{3,2,1,0:T(1,128)S(1)} collective-permute-done((f32[3,18,1,128]{3,2,1,0:T(1,128)S(1)}, f32[3,18,1,128]{3,2,1,0:T(1,128)S(1)}, u32[]{:S(2)}, u32[]{:S(2)}) %collective-permute-start.14) | collective-permute-done | bytes 27680 | tf_op jit(solution)/shard_map/ppermute | solution.py:16
  121.7 0.3 pad_maximum_fusion.7
  122.0 0.6 fusion.167
  122.7 0.4 maximum_maximum_fusion.3
  123.0 7.3 %fusion.4 = bf16[3,16,64,128]{3,2,1,0:T(8,128)(2,1)} fusion(f32[3,16,64,128]{3,2,1,0:T(8,128)S(1)} %fusion.38, f32[3,18,66,64]{3,2,1,0:T(8,128)S(1)} %get-tuple-element.9, f32[3,18,66,64]{3,2,1,0:T(8,128)S(1)} %get-tuple-element.8, f32[3,18,65,128]{3,2,1,0:T(8,128)S(1)} %get-tuple-element.17, f32[3,1,64,128]{3,2,1,0:T(8,128)S(1)} %collective-permute-done.13, ...), kind=kLoop, calls=%fused_computation.17 | loop fusion | flops 20054016 | bytes 24827904 | tf_op jit(solution)/shard_map/convert_element_type | solution.py:75
  130.3 3.2 %reshape.116 = bf16[3072,2,64]{2,1,0:T(2,128)(2,1)S(1)} reshape(bf16[3,16,64,128]{3,2,1,0:T(8,128)(2,1)} %fusion.4) | data formatting | bytes 1572864 | tf_op jit(solution)/shard_map/reshape | solution.py:77
  133.5 3.1 %fusion.171 = (bf16[3072,1,64]{2,1,0:T(2,128)(2,1)S(1)}, bf16[3072,1,64]{2,1,0:T(2,128)(2,1)}) fusion(bf16[3072,2,64]{2,1,0:T(2,128)(2,1)S(1)} %reshape.116), kind=kLoop, calls=%fused_computation.398 | loop fusion | bytes 1572864 | tf_op jit(solution)/shard_map/slice | solution.py:62
  136.6 3.5 %copy.17 = bf16[3072,1,64]{0,2,1:T(8,128)(2,1)S(1)} copy(bf16[3072,1,64]{2,1,0:T(2,128)(2,1)} %get-tuple-element.41) | data formatting | bytes 786432
  140.1 1.5 copy.19
  141.6 0.3 fusion.164
  141.9 0.2 fusion.137
  142.2 71.9 %all-reduce = f32[64,64]{0,1:T(8,128)S(1)} all-reduce(f32[64,64]{0,1:T(8,128)S(1)} %fusion.137), channel_id=2, replica_groups=mesh['gx'=16,'gz'=16] {'gx'}, use_global_device_ids=true, to_apply=%region_1.2.clone | all-reduce | flops 4096 | bytes 32768
  214.1 52.9 %psum.8 = f32[4,64]{0,1:T(8,128)S(1)} all-reduce(f32[4,64]{0,1:T(8,128)S(1)} %constant_dynamic-slice_fusion), channel_id=1, replica_groups=mesh['gx'=16,'gz'=16] {'gz'}, use_global_device_ids=true, to_apply=%region_0.1 | all-reduce | flops 256 | bytes 2048 | tf_op jit(solution)/shard_map/psum | solution.py:79
  267.1 0.7 copy.12
  (126 shorter events, 3.3 us)
Async XLA Ops:
  0.6 10.3 %copy-start.20 = (f32[36,16,64]{2,1,0:T(8,128)S(1)}, f32[36,16,64]{2,1,0:T(8,128)}, u32[]{:S(2)}) copy-start(f32[36,16,64]{2,1,0:T(8,128)} %param.6) | copy-start | bytes 442372
  2.2 10.1 %copy-start.21 = (f32[18,16,64]{2,1,0:T(8,128)S(1)}, f32[18,16,64]{2,1,0:T(8,128)}, u32[]{:S(2)}) copy-start(f32[18,16,64]{2,1,0:T(8,128)} %param.7) | copy-start | bytes 221188
  2.2 28.2 %collective-permute-start.1 = (f32[3,1,64,128]{3,2,1,0:T(8,128)}, f32[3,1,64,128]{3,2,1,0:T(8,128)S(1)}, u32[]{:S(2)}, u32[]{:S(2)}) collective-permute-start(f32[3,1,64,128]{3,2,1,0:T(8,128)} %get-tuple-element.51), channel_id=1, source_target_pairs={{16,0},{32,16},{48,32},{64,48},{80,64},{96,80},{112,96},{128,112},... | collective-permute-start | bytes 294920 | tf_op jit(solution)/shard_map/ppermute | solution.py:17
  9.6 20.8 %collective-permute-start = (f32[3,1,64,128]{3,2,1,0:T(8,128)}, f32[3,1,64,128]{3,2,1,0:T(8,128)S(1)}, u32[]{:S(2)}, u32[]{:S(2)}) collective-permute-start(f32[3,1,64,128]{3,2,1,0:T(8,128)} %get-tuple-element.50), channel_id=1, source_target_pairs={{0,16},{16,32},{32,48},{48,64},{64,80},{80,96},{96,112},{112,128},... | collective-permute-start | bytes 294920 | tf_op jit(solution)/shard_map/ppermute | solution.py:16
  15.6 3.6 %copy-start.33 = (f32[16,64]{1,0:T(8,128)S(1)}, f32[16,64]{1,0:T(8,128)}, u32[]{:S(2)}) copy-start(f32[16,64]{1,0:T(8,128)} %get-tuple-element.53) | copy-start | bytes 12292
  15.6 3.6 %copy-start.34 = (f32[16,64]{1,0:T(8,128)S(1)}, f32[16,64]{1,0:T(8,128)}, u32[]{:S(2)}) copy-start(f32[16,64]{1,0:T(8,128)} %get-tuple-element.54) | copy-start | bytes 12292
  15.6 3.6 %copy-start.35 = (f32[16,64]{1,0:T(8,128)S(1)}, f32[16,64]{1,0:T(8,128)}, u32[]{:S(2)}) copy-start(f32[16,64]{1,0:T(8,128)} %get-tuple-element.55) | copy-start | bytes 12292
  15.6 3.6 %copy-start.36 = (f32[16,64]{1,0:T(8,128)S(1)}, f32[16,64]{1,0:T(8,128)}, u32[]{:S(2)}) copy-start(f32[16,64]{1,0:T(8,128)} %get-tuple-element.56) | copy-start | bytes 12292
  15.6 3.6 %copy-start.37 = (f32[16,64]{1,0:T(8,128)S(1)}, f32[16,64]{1,0:T(8,128)}, u32[]{:S(2)}) copy-start(f32[16,64]{1,0:T(8,128)} %get-tuple-element.57) | copy-start | bytes 12292
  15.6 3.6 %copy-start.38 = (f32[16,64]{1,0:T(8,128)S(1)}, f32[16,64]{1,0:T(8,128)}, u32[]{:S(2)}) copy-start(f32[16,64]{1,0:T(8,128)} %get-tuple-element.58) | copy-start | bytes 12292
  15.6 3.6 %copy-start.39 = (f32[16,64]{1,0:T(8,128)S(1)}, f32[16,64]{1,0:T(8,128)}, u32[]{:S(2)}) copy-start(f32[16,64]{1,0:T(8,128)} %get-tuple-element.59) | copy-start | bytes 12292
  15.6 3.6 %copy-start.40 = (f32[16,64]{1,0:T(8,128)S(1)}, f32[16,64]{1,0:T(8,128)}, u32[]{:S(2)}) copy-start(f32[16,64]{1,0:T(8,128)} %get-tuple-element.60) | copy-start | bytes 12292
  15.6 3.6 %copy-start.41 = (f32[16,64]{1,0:T(8,128)S(1)}, f32[16,64]{1,0:T(8,128)}, u32[]{:S(2)}) copy-start(f32[16,64]{1,0:T(8,128)} %get-tuple-element.61) | copy-start | bytes 12292
  15.7 3.6 %copy-start.42 = (f32[16,64]{1,0:T(8,128)S(1)}, f32[16,64]{1,0:T(8,128)}, u32[]{:S(2)}) copy-start(f32[16,64]{1,0:T(8,128)} %get-tuple-element.62) | copy-start | bytes 12292
  15.7 3.6 %copy-start.43 = (f32[16,64]{1,0:T(8,128)S(1)}, f32[16,64]{1,0:T(8,128)}, u32[]{:S(2)}) copy-start(f32[16,64]{1,0:T(8,128)} %get-tuple-element.63) | copy-start | bytes 12292
  15.7 3.6 %copy-start.44 = (f32[16,64]{1,0:T(8,128)S(1)}, f32[16,64]{1,0:T(8,128)}, u32[]{:S(2)}) copy-start(f32[16,64]{1,0:T(8,128)} %get-tuple-element.64) | copy-start | bytes 12292
  15.7 3.6 %copy-start.45 = (f32[16,64]{1,0:T(8,128)S(1)}, f32[16,64]{1,0:T(8,128)}, u32[]{:S(2)}) copy-start(f32[16,64]{1,0:T(8,128)} %get-tuple-element.65) | copy-start | bytes 12292
  15.7 3.6 %copy-start.46 = (f32[16,64]{1,0:T(8,128)S(1)}, f32[16,64]{1,0:T(8,128)}, u32[]{:S(2)}) copy-start(f32[16,64]{1,0:T(8,128)} %get-tuple-element.66) | copy-start | bytes 12292
  15.7 3.6 %copy-start.47 = (f32[16,64]{1,0:T(8,128)S(1)}, f32[16,64]{1,0:T(8,128)}, u32[]{:S(2)}) copy-start(f32[16,64]{1,0:T(8,128)} %get-tuple-element.67) | copy-start | bytes 12292
  15.7 3.6 %copy-start.48 = (f32[16,64]{1,0:T(8,128)S(1)}, f32[16,64]{1,0:T(8,128)}, u32[]{:S(2)}) copy-start(f32[16,64]{1,0:T(8,128)} %get-tuple-element.68) | copy-start | bytes 12292
  15.7 3.6 %copy-start.49 = (f32[16,64]{1,0:T(8,128)S(1)}, f32[16,64]{1,0:T(8,128)}, u32[]{:S(2)}) copy-start(f32[16,64]{1,0:T(8,128)} %get-tuple-element.86) | copy-start | bytes 12292
  15.7 3.6 %copy-start.50 = (f32[16,64]{1,0:T(8,128)S(1)}, f32[16,64]{1,0:T(8,128)}, u32[]{:S(2)}) copy-start(f32[16,64]{1,0:T(8,128)} %get-tuple-element.87) | copy-start | bytes 12292
  19.4 4.0 %copy-start.22 = (f32[16,64]{1,0:T(8,128)S(1)}, f32[16,64]{1,0:T(8,128)}, u32[]{:S(2)}) copy-start(f32[16,64]{1,0:T(8,128)} %get-tuple-element.75) | copy-start | bytes 12292
  19.4 4.0 %copy-start.23 = (f32[16,64]{1,0:T(8,128)S(1)}, f32[16,64]{1,0:T(8,128)}, u32[]{:S(2)}) copy-start(f32[16,64]{1,0:T(8,128)} %get-tuple-element.76) | copy-start | bytes 12292
  19.4 4.0 %copy-start.24 = (f32[16,64]{1,0:T(8,128)S(1)}, f32[16,64]{1,0:T(8,128)}, u32[]{:S(2)}) copy-start(f32[16,64]{1,0:T(8,128)} %get-tuple-element.77) | copy-start | bytes 12292
  19.4 4.0 %copy-start.25 = (f32[16,64]{1,0:T(8,128)S(1)}, f32[16,64]{1,0:T(8,128)}, u32[]{:S(2)}) copy-start(f32[16,64]{1,0:T(8,128)} %get-tuple-element.78) | copy-start | bytes 12292
  19.4 4.0 %copy-start.26 = (f32[16,64]{1,0:T(8,128)S(1)}, f32[16,64]{1,0:T(8,128)}, u32[]{:S(2)}) copy-start(f32[16,64]{1,0:T(8,128)} %get-tuple-element.79) | copy-start | bytes 12292
  19.4 4.0 %copy-start.27 = (f32[16,64]{1,0:T(8,128)S(1)}, f32[16,64]{1,0:T(8,128)}, u32[]{:S(2)}) copy-start(f32[16,64]{1,0:T(8,128)} %get-tuple-element.80) | copy-start | bytes 12292
  19.4 4.0 %copy-start.28 = (f32[16,64]{1,0:T(8,128)S(1)}, f32[16,64]{1,0:T(8,128)}, u32[]{:S(2)}) copy-start(f32[16,64]{1,0:T(8,128)} %get-tuple-element.81) | copy-start | bytes 12292
  19.4 4.0 %copy-start.29 = (f32[16,64]{1,0:T(8,128)S(1)}, f32[16,64]{1,0:T(8,128)}, u32[]{:S(2)}) copy-start(f32[16,64]{1,0:T(8,128)} %get-tuple-element.82) | copy-start | bytes 12292
  19.4 4.0 %copy-start.30 = (f32[16,64]{1,0:T(8,128)S(1)}, f32[16,64]{1,0:T(8,128)}, u32[]{:S(2)}) copy-start(f32[16,64]{1,0:T(8,128)} %get-tuple-element.83) | copy-start | bytes 12292
  19.4 4.0 %copy-start.31 = (f32[16,64]{1,0:T(8,128)S(1)}, f32[16,64]{1,0:T(8,128)}, u32[]{:S(2)}) copy-start(f32[16,64]{1,0:T(8,128)} %get-tuple-element.84) | copy-start | bytes 12292
  19.5 4.0 %copy-start.32 = (f32[16,64]{1,0:T(8,128)S(1)}, f32[16,64]{1,0:T(8,128)}, u32[]{:S(2)}) copy-start(f32[16,64]{1,0:T(8,128)} %get-tuple-element.85) | copy-start | bytes 12292
  31.1 14.1 %collective-permute-start.3 = (f32[3,18,1,128]{3,2,1,0:T(1,128)}, f32[3,18,1,128]{3,2,1,0:T(1,128)S(1)}, u32[]{:S(2)}, u32[]{:S(2)}) collective-permute-start(f32[3,18,1,128]{3,2,1,0:T(1,128)} %get-tuple-element.31), channel_id=1, source_target_pairs={{1,0},{2,1},{3,2},{4,3},{5,4},{6,5},{7,6},{8,7},{9,8},{10,9},{11,1... | collective-permute-start | bytes 82952 | tf_op jit(solution)/shard_map/ppermute | solution.py:17
  34.1 11.1 %collective-permute-start.2 = (f32[3,18,1,128]{3,2,1,0:T(1,128)}, f32[3,18,1,128]{3,2,1,0:T(1,128)S(1)}, u32[]{:S(2)}, u32[]{:S(2)}) collective-permute-start(f32[3,18,1,128]{3,2,1,0:T(1,128)} %get-tuple-element.30), channel_id=1, source_target_pairs={{0,1},{1,2},{2,3},{3,4},{4,5},{5,6},{6,7},{7,8},{8,9},{9,10},{10,1... | collective-permute-start | bytes 82952 | tf_op jit(solution)/shard_map/ppermute | solution.py:16
  35.8 8.2 %copy-start.51 = (u32[256]{0:T(256)S(1)}, u32[256]{0:T(256)}, u32[]{:S(2)}) copy-start(u32[256]{0:T(256)} %constant.4) | copy-start | bytes 3076
  45.6 1.6 copy-start.15
  45.6 1.8 copy-start.16
  45.6 1.9 copy-start.17
  46.3 1.6 copy-start
  46.3 1.8 copy-start.1
  46.3 1.9 copy-start.2
  46.3 2.1 copy-start.3
  46.3 2.2 copy-start.4
  46.3 2.3 copy-start.5
  46.3 2.5 copy-start.6
  46.3 2.6 copy-start.7
  46.3 2.8 %copy-start.8 = (f32[16,64,128]{2,1,0:T(8,128)S(1)}, f32[16,64,128]{2,1,0:T(8,128)}, u32[]{:S(2)}) copy-start(f32[16,64,128]{2,1,0:T(8,128)} %get-tuple-element.108) | copy-start | bytes 1572868
  46.3 2.9 %copy-start.9 = (f32[16,64,128]{2,1,0:T(8,128)S(1)}, f32[16,64,128]{2,1,0:T(8,128)}, u32[]{:S(2)}) copy-start(f32[16,64,128]{2,1,0:T(8,128)} %get-tuple-element.109) | copy-start | bytes 1572868
  46.4 3.1 %copy-start.10 = (f32[16,64,128]{2,1,0:T(8,128)S(1)}, f32[16,64,128]{2,1,0:T(8,128)}, u32[]{:S(2)}) copy-start(f32[16,64,128]{2,1,0:T(8,128)} %get-tuple-element.110) | copy-start | bytes 1572868
  55.9 7.2 %collective-permute-start.5 = (f32[3,1,64,128]{3,2,1,0:T(8,128)S(1)}, f32[3,1,64,128]{3,2,1,0:T(8,128)S(1)}, u32[]{:S(2)}, u32[]{:S(2)}) collective-permute-start(f32[3,1,64,128]{3,2,1,0:T(8,128)S(1)} %get-tuple-element.49), channel_id=1, source_target_pairs={{16,0},{32,16},{48,32},{64,48},{80,64},{96,80},{112,96},{128,112},... | collective-permute-start | bytes 294920 | tf_op jit(solution)/shard_map/ppermute | solution.py:17
  60.9 8.2 %collective-permute-start.4 = (f32[3,1,64,128]{3,2,1,0:T(8,128)S(1)}, f32[3,1,64,128]{3,2,1,0:T(8,128)S(1)}, u32[]{:S(2)}, u32[]{:S(2)}) collective-permute-start(f32[3,1,64,128]{3,2,1,0:T(8,128)S(1)} %get-tuple-element.48), channel_id=1, source_target_pairs={{0,16},{16,32},{32,48},{48,64},{64,80},{80,96},{96,112},{112,128},... | collective-permute-start | bytes 294920 | tf_op jit(solution)/shard_map/ppermute | solution.py:16
  69.1 4.7 %collective-permute-start.7 = (f32[3,18,1,128]{3,2,1,0:T(1,128)S(1)}, f32[3,18,1,128]{3,2,1,0:T(1,128)S(1)}, u32[]{:S(2)}, u32[]{:S(2)}) collective-permute-start(f32[3,18,1,128]{3,2,1,0:T(1,128)S(1)} %get-tuple-element.27), channel_id=1, source_target_pairs={{1,0},{2,1},{3,2},{4,3},{5,4},{6,5},{7,6},{8,7},{9,8},{10,9},{11,1... | collective-permute-start | bytes 82952 | tf_op jit(solution)/shard_map/ppermute | solution.py:17
  72.2 5.4 %collective-permute-start.6 = (f32[3,18,1,128]{3,2,1,0:T(1,128)S(1)}, f32[3,18,1,128]{3,2,1,0:T(1,128)S(1)}, u32[]{:S(2)}, u32[]{:S(2)}) collective-permute-start(f32[3,18,1,128]{3,2,1,0:T(1,128)S(1)} %get-tuple-element.26), channel_id=1, source_target_pairs={{0,1},{1,2},{2,3},{3,4},{4,5},{5,6},{6,7},{7,8},{8,9},{9,10},{10,1... | collective-permute-start | bytes 82952 | tf_op jit(solution)/shard_map/ppermute | solution.py:16
  85.4 4.7 %collective-permute-start.9 = (f32[3,1,64,128]{3,2,1,0:T(8,128)S(1)}, f32[3,1,64,128]{3,2,1,0:T(8,128)S(1)}, u32[]{:S(2)}, u32[]{:S(2)}) collective-permute-start(f32[3,1,64,128]{3,2,1,0:T(8,128)S(1)} %get-tuple-element.47), channel_id=1, source_target_pairs={{16,0},{32,16},{48,32},{64,48},{80,64},{96,80},{112,96},{128,112},... | collective-permute-start | bytes 294920 | tf_op jit(solution)/shard_map/ppermute | solution.py:17
  85.5 8.3 %collective-permute-start.8 = (f32[3,1,64,128]{3,2,1,0:T(8,128)S(1)}, f32[3,1,64,128]{3,2,1,0:T(8,128)S(1)}, u32[]{:S(2)}, u32[]{:S(2)}) collective-permute-start(f32[3,1,64,128]{3,2,1,0:T(8,128)S(1)} %get-tuple-element.46), channel_id=1, source_target_pairs={{0,16},{16,32},{32,48},{48,64},{64,80},{80,96},{96,112},{112,128},... | collective-permute-start | bytes 294920 | tf_op jit(solution)/shard_map/ppermute | solution.py:16
  93.9 1.6 collective-permute-start.11
  94.0 5.7 %collective-permute-start.10 = (f32[3,18,1,128]{3,2,1,0:T(1,128)S(1)}, f32[3,18,1,128]{3,2,1,0:T(1,128)S(1)}, u32[]{:S(2)}, u32[]{:S(2)}) collective-permute-start(f32[3,18,1,128]{3,2,1,0:T(1,128)S(1)} %get-tuple-element.22), channel_id=1, source_target_pairs={{0,1},{1,2},{2,3},{3,4},{4,5},{5,6},{6,7},{7,8},{8,9},{9,10},{10,1... | collective-permute-start | bytes 82952 | tf_op jit(solution)/shard_map/ppermute | solution.py:16
  107.5 4.7 %collective-permute-start.13 = (f32[3,1,64,128]{3,2,1,0:T(8,128)S(1)}, f32[3,1,64,128]{3,2,1,0:T(8,128)S(1)}, u32[]{:S(2)}, u32[]{:S(2)}) collective-permute-start(f32[3,1,64,128]{3,2,1,0:T(8,128)S(1)} %get-tuple-element.45), channel_id=1, source_target_pairs={{16,0},{32,16},{48,32},{64,48},{80,64},{96,80},{112,96},{128,112},... | collective-permute-start | bytes 294920 | tf_op jit(solution)/shard_map/ppermute | solution.py:17
  107.6 8.3 %collective-permute-start.12 = (f32[3,1,64,128]{3,2,1,0:T(8,128)S(1)}, f32[3,1,64,128]{3,2,1,0:T(8,128)S(1)}, u32[]{:S(2)}, u32[]{:S(2)}) collective-permute-start(f32[3,1,64,128]{3,2,1,0:T(8,128)S(1)} %get-tuple-element.44), channel_id=1, source_target_pairs={{0,16},{16,32},{32,48},{48,64},{64,80},{80,96},{96,112},{112,128},... | collective-permute-start | bytes 294920 | tf_op jit(solution)/shard_map/ppermute | solution.py:16
  115.9 1.6 collective-permute-start.15
  116.0 5.7 %collective-permute-start.14 = (f32[3,18,1,128]{3,2,1,0:T(1,128)S(1)}, f32[3,18,1,128]{3,2,1,0:T(1,128)S(1)}, u32[]{:S(2)}, u32[]{:S(2)}) collective-permute-start(f32[3,18,1,128]{3,2,1,0:T(1,128)S(1)} %get-tuple-element.18), channel_id=1, source_target_pairs={{0,1},{1,2},{2,3},{3,4},{4,5},{5,6},{6,7},{7,8},{8,9},{9,10},{10,1... | collective-permute-start | bytes 82952 | tf_op jit(solution)/shard_map/ppermute | solution.py:16
  136.6 5.1 %copy-start.18 = (bf16[3072,1,64]{0,2,1:T(8,128)(2,1)S(1)}, bf16[3072,1,64]{0,2,1:T(8,128)(2,1)}, u32[]{:S(2)}) copy-start(bf16[3072,1,64]{0,2,1:T(8,128)(2,1)} %copy.18) | copy-start | bytes 1179652
  140.1 1.8 copy-start.19
  (4 other events, 5.2 us)
where the time goes:
time: 268 us
  blocking collectives  125 us (47%)
  other arithmetic  52.6 us (20%)
  local copies, waits for them, and re-layouts  35.8 us (13%)
  waiting for transfers between devices  27.8 us (10%)
  starting transfers between devices  23.9 us (9%)
    unnamed x1, blocking collectives  71.9 us
    psum x1, blocking collectives, body(): spanned = lax.psum(partial_sum, 'gz')  52.9 us
    ppermute x8, waiting for transfers between devices, with_halo(): before = lax.ppermute(last, axis, up)  25.6 us
    add x3, other arithmetic, advance(): return own + total + jnp.stack(mixed, axis=0)  19.4 us
    ppermute x8, starting transfers between devices, with_halo(): after = lax.ppermute(leading, axis, down)  18.9 us
    unnamed x111, local copies, waits for them, and re-layouts  17.3 us
    add x8, other arithmetic, advance(): term = term + weight * own[other_at]  13.3 us
    select_n x2, other arithmetic, lane_weight(): return jnp.where(lower, first[:, :, None], second[:, :, None])  7.98 us
  transfers between devices with their start and end apart: 16, of which 12 were waited for; matrix products, arithmetic and copies ran while one was open for 15% of the time, Pallas kernels for 0%

commit v1 on v0

--- a/solution.py
+++ b/solution.py
@@ -76,7 +76,7 @@
     adjoint_flat = adjoint_modes.reshape(-1, 2, modes)
     evolved_flat = evolved.reshape(-1, 2, modes)
     partial_sum = plane_product(adjoint_flat, evolved_flat)
-    spanned = lax.psum(partial_sum, "gz")
+    spanned = jnp.sum(lax.all_gather(partial_sum, "gz"), axis=0)
     reduced = lax.psum_scatter(spanned, "gx", scatter_dimension=0, tiled=True)
     return (evolved, reduced)
 

time: 268 us -> 234 us (0.87)
  blocking collectives: 125 us -> 89.4 us
    psum x1 -> x0, blocking collectives: 52.9 us -> none  [body(): spanned = lax.psum(partial_sum, 'gz')]
    all_gather x0 -> x1, blocking collectives: none -> 17.5 us  [body(): spanned = jnp.sum(lax.all_gather(partial_sum, 'gz'), axis=0)]
    unnamed x111 -> x110, local copies, waits for them, and re-layouts: 17.3 us -> 17.2 us
  transfers between devices with their start and end apart: 16 -> 16, of which waited for: 12 -> 12; matrix products, arithmetic and copies ran while one was open for 15% -> 17% of each run, Pallas kernels for 0% -> 0%
where the time goes in v1:
time: 234 us; the launch traced here: 232 us
  blocking collectives  89.4 us (38%)
  other arithmetic  52.6 us (22%)
  local copies, waits for them, and re-layouts  35.7 us (15%)
  waiting for transfers between devices  27.8 us (12%)
  starting transfers between devices  23.9 us (10%)
    unnamed x1, blocking collectives  71.9 us
    ppermute x8, waiting for transfers between devices, with_halo(): before = lax.ppermute(last, axis, up)  25.6 us
    add x3, other arithmetic, advance(): return own + total + jnp.stack(mixed, axis=0)  19.4 us
    ppermute x8, starting transfers between devices, with_halo(): after = lax.ppermute(leading, axis, down)  18.9 us
    all_gather x1, blocking collectives, body(): spanned = jnp.sum(lax.all_gather(partial_sum, 'gz'), axis=0)  17.5 us
    unnamed x110, local copies, waits for them, and re-layouts  17.2 us
    add x8, other arithmetic, advance(): term = term + weight * own[other_at]  13.3 us
    select_n x2, other arithmetic, lane_weight(): return jnp.where(lower, first[:, :, None], second[:, :, None])  7.98 us
  transfers between devices with their start and end apart: 16, of which 12 were waited for; matrix products, arithmetic and copies ran while one was open for 17% of the time, Pallas kernels for 0%

profile of v1, /device:TPU:2, one launch (start us, length us, event | category | flops | bytes accessed | tf_op | source)
XLA Modules:
  0.0 232.3 jit_solution(2216094166910237078)
XLA Ops:
  0.6 1.6 fusion.176
  2.2 7.4 %collective-permute-start.1 = (f32[3,1,64,128]{3,2,1,0:T(8,128)}, f32[3,1,64,128]{3,2,1,0:T(8,128)S(1)}, u32[]{:S(2)}, u32[]{:S(2)}) collective-permute-start(f32[3,1,64,128]{3,2,1,0:T(8,128)} %get-tuple-element.45), channel_id=1, source_target_pairs={{16,0},{32,16},{48,32},{64,48},{80,64},{96,80},{112,96},{128,112},... | collective-permute-start | bytes 294920 | tf_op jit(solution)/shard_map/ppermute | solution.py:17
  9.6 1.3 convert_element_type.6
  10.9 0.7 slice_bitcast_fusion.53
  11.6 0.7 slice_bitcast_fusion.52
  12.3 3.2 %reshape.118 = bf16[3072,2,64]{2,1,0:T(2,128)(2,1)S(1)} reshape(bf16[3,16,64,128]{3,2,1,0:T(8,128)(2,1)} %param.5) | data formatting | bytes 1572864 | tf_op jit(solution)/shard_map/reshape | solution.py:76
  15.7 3.5 %fusion.172 = (bf16[3072,1,64]{2,1,0:T(2,128)(2,1)}, bf16[3072,1,64]{2,1,0:T(2,128)(2,1)}) fusion(bf16[3072,2,64]{2,1,0:T(2,128)(2,1)S(1)} %reshape.118), kind=kLoop, calls=%fused_computation.399 | loop fusion | bytes 1572864 | tf_op jit(solution)/shard_map/slice | solution.py:61
  19.5 3.9 %broadcast_select_fusion.8 = (f32[16,64,128]{2,1,0:T(8,128)S(1)}, f32[16,64,128]{2,1,0:T(8,128)S(1)}, f32[16,64,128]{2,1,0:T(8,128)S(1)}, f32[16,64,128]{2,1,0:T...) fusion(f32[16,64]{1,0:T(8,128)S(1)} %copy-done.47, ...), kind=kLoop, calls=%fused_computation.316 | loop fusion | flops 1179648 | bytes 4792448 | tf_op jit(solution)/shard_map/jit(_where)/select_n | solution.py:23
  23.4 4.1 %broadcast_select_fusion.17 = (f32[16,64,128]{2,1,0:T(8,128)}, f32[16,64,128]{2,1,0:T(8,128)}, f32[16,64,128]{2,1,0:T(8,128)}, f32[16,64,128]{2,1,0:T(8,128)}, f...) fusion(f32[16,64]{1,0:T(8,128)S(1)} %get-tuple-element.65, ...), kind=kLoop, calls=%fused_computation.325 | loop fusion | flops 1179648 | bytes 4792448 | tf_op jit(solution)/shard_map/jit(_where)/select_n | solution.py:23
  27.6 2.9 %fusion.139 = (f32[1,16,64,128]{3,2,1,0:T(8,128)}, f32[1,16,64,128]{3,2,1,0:T(8,128)}) fusion(f32[3,16,64,128]{3,2,1,0:T(8,128)S(1)} %convert_element_type.6, f32[16,64]{1,0:T(8,128)S(1)} %get-tuple-element.93, f32[16,64]{1,0:T(8,128)S(1)} %get-tuple-element.94, f32[16,64]{1,0:T(8,128)S(1)} %get-tuple-element.95, f32[16,64]{1,0:T(8,128)S(1)} %get-tuple-element.96, ...), kind=kLoop, calls=%fused_computation.280 | loop fusion | flops 2097152 | bytes 2670720 | tf_op jit(solution)/shard_map/add | solution.py:52
  30.4 0.7 pad_maximum_fusion.31
  31.1 3.0 %collective-permute-start.3 = (f32[3,18,1,128]{3,2,1,0:T(1,128)}, f32[3,18,1,128]{3,2,1,0:T(1,128)S(1)}, u32[]{:S(2)}, u32[]{:S(2)}) collective-permute-start(f32[3,18,1,128]{3,2,1,0:T(1,128)} %get-tuple-element.25), channel_id=1, source_target_pairs={{1,0},{2,1},{3,2},{4,3},{5,4},{6,5},{7,6},{8,7},{9,8},{10,9},{11,1... | collective-permute-start | bytes 82952 | tf_op jit(solution)/shard_map/ppermute | solution.py:17
  34.1 1.7 fusion.155
  35.8 4.1 %copy.17 = bf16[3072,1,64]{0,2,1:T(8,128)(2,1)} copy(bf16[3072,1,64]{2,1,0:T(2,128)(2,1)} %get-tuple-element.37) | data formatting | bytes 786432
  39.9 4.1 %copy.19 = bf16[3072,1,64]{0,2,1:T(8,128)(2,1)} copy(bf16[3072,1,64]{2,1,0:T(2,128)(2,1)} %get-tuple-element.36) | data formatting | bytes 786432
  44.0 0.6 dynamic-slice
  45.3 0.3 pad_maximum_fusion.1
  45.6 0.6 fusion.170
  46.4 0.4 maximum_maximum_fusion
  47.5 0.3 copy-done
  49.4 6.4 %fusion.106 = f32[3,16,64,128]{3,2,1,0:T(8,128)S(1)} fusion(f32[3,16,64,128]{3,2,1,0:T(8,128)S(1)} %convert_element_type.6, f32[3,18,66,64]{3,2,1,0:T(8,128)S(1)} %get-tuple-element.9, f32[3,18,66,64]{3,2,1,0:T(8,128)S(1)} %get-tuple-element.8, f32[3,18,65,128]{3,2,1,0:T(8,128)S(1)} %get-tuple-element.23, f32[3,1,64,128]{3,2,1,0:T(8,128)S(1)} %collective-permute-done.1, ...), kind=kLoop, calls=%fused_computation.188 | loop fusion | flops 19660800 | bytes 25614336 | tf_op jit(solution)/shard_map/add | solution.py:54
  55.9 5.0 %collective-permute-start.5 = (f32[3,1,64,128]{3,2,1,0:T(8,128)S(1)}, f32[3,1,64,128]{3,2,1,0:T(8,128)S(1)}, u32[]{:S(2)}, u32[]{:S(2)}) collective-permute-start(f32[3,1,64,128]{3,2,1,0:T(8,128)S(1)} %get-tuple-element.43), channel_id=1, source_target_pairs={{16,0},{32,16},{48,32},{64,48},{80,64},{96,80},{112,96},{128,112},... | collective-permute-start | bytes 294920 | tf_op jit(solution)/shard_map/ppermute | solution.py:17
  60.9 2.0 fusion.141
  62.8 0.3 collective-permute-done.5
  63.1 6.0 %collective-permute-done.4 = f32[3,1,64,128]{3,2,1,0:T(8,128)S(1)} collective-permute-done((f32[3,1,64,128]{3,2,1,0:T(8,128)S(1)}, f32[3,1,64,128]{3,2,1,0:T(8,128)S(1)}, u32[]{:S(2)}, u32[]{:S(2)}) %collective-permute-start.4) | collective-permute-done | bytes 98336 | tf_op jit(solution)/shard_map/ppermute | solution.py:16
  69.1 3.1 %collective-permute-start.7 = (f32[3,18,1,128]{3,2,1,0:T(1,128)S(1)}, f32[3,18,1,128]{3,2,1,0:T(1,128)S(1)}, u32[]{:S(2)}, u32[]{:S(2)}) collective-permute-start(f32[3,18,1,128]{3,2,1,0:T(1,128)S(1)} %get-tuple-element.21), channel_id=1, source_target_pairs={{1,0},{2,1},{3,2},{4,3},{5,4},{6,5},{7,6},{8,7},{9,8},{10,9},{11,1... | collective-permute-start | bytes 82952 | tf_op jit(solution)/shard_map/ppermute | solution.py:17
  72.2 1.0 fusion.157
  73.2 0.6 collective-permute-done.7
  73.8 3.8 %collective-permute-done.6 = f32[3,18,1,128]{3,2,1,0:T(1,128)S(1)} collective-permute-done((f32[3,18,1,128]{3,2,1,0:T(1,128)S(1)}, f32[3,18,1,128]{3,2,1,0:T(1,128)S(1)}, u32[]{:S(2)}, u32[]{:S(2)}) %collective-permute-start.6) | collective-permute-done | bytes 27680 | tf_op jit(solution)/shard_map/ppermute | solution.py:16
  77.6 0.3 pad_maximum_fusion.3
  77.9 0.6 fusion.169
  78.6 0.4 maximum_maximum_fusion.1
  78.9 6.5 %fusion.72 = f32[3,16,64,128]{3,2,1,0:T(8,128)S(1)} fusion(f32[3,16,64,128]{3,2,1,0:T(8,128)S(1)} %fusion.106, f32[3,18,66,64]{3,2,1,0:T(8,128)S(1)} %get-tuple-element.7, f32[3,18,66,64]{3,2,1,0:T(8,128)S(1)} %get-tuple-element.6, f32[3,18,65,128]{3,2,1,0:T(8,128)S(1)} %get-tuple-element.19, f32[3,1,64,128]{3,2,1,0:T(8,128)S(1)} %collective-permute-done.5, ...), kind=kLoop, calls=%fused_computation.131 | loop fusion | flops 19660800 | bytes 25614336 | tf_op jit(solution)/shard_map/add | solution.py:54
  85.5 2.0 collective-permute-start.8
  87.5 2.0 fusion.143
  89.5 0.6 collective-permute-done.9
  90.1 3.7 %collective-permute-done.8 = f32[3,1,64,128]{3,2,1,0:T(8,128)S(1)} collective-permute-done((f32[3,1,64,128]{3,2,1,0:T(8,128)S(1)}, f32[3,1,64,128]{3,2,1,0:T(8,128)S(1)}, u32[]{:S(2)}, u32[]{:S(2)}) %collective-permute-start.8) | collective-permute-done | bytes 98336 | tf_op jit(solution)/shard_map/ppermute | solution.py:16
  94.0 0.5 collective-permute-start.10
  94.5 1.0 fusion.159
  95.5 4.1 %collective-permute-done.10 = f32[3,18,1,128]{3,2,1,0:T(1,128)S(1)} collective-permute-done((f32[3,18,1,128]{3,2,1,0:T(1,128)S(1)}, f32[3,18,1,128]{3,2,1,0:T(1,128)S(1)}, u32[]{:S(2)}, u32[]{:S(2)}) %collective-permute-start.10) | collective-permute-done | bytes 27680 | tf_op jit(solution)/shard_map/ppermute | solution.py:16
  99.7 0.3 pad_maximum_fusion.5
  99.9 0.6 fusion.168
  100.6 0.4 maximum_maximum_fusion.2
  101.0 6.5 %fusion.38 = f32[3,16,64,128]{3,2,1,0:T(8,128)S(1)} fusion(f32[3,16,64,128]{3,2,1,0:T(8,128)S(1)} %fusion.72, f32[3,18,66,64]{3,2,1,0:T(8,128)S(1)} %get-tuple-element.5, f32[3,18,66,64]{3,2,1,0:T(8,128)S(1)} %get-tuple-element.4, f32[3,18,65,128]{3,2,1,0:T(8,128)S(1)} %get-tuple-element.15, f32[3,1,64,128]{3,2,1,0:T(8,128)S(1)} %collective-permute-done.9, ...), kind=kLoop, calls=%fused_computation.74 | loop fusion | flops 19660800 | bytes 25614336 | tf_op jit(solution)/shard_map/add | solution.py:54
  107.6 2.0 collective-permute-start.12
  109.6 2.0 fusion.145
  111.5 0.6 collective-permute-done.13
  112.2 3.7 %collective-permute-done.12 = f32[3,1,64,128]{3,2,1,0:T(8,128)S(1)} collective-permute-done((f32[3,1,64,128]{3,2,1,0:T(8,128)S(1)}, f32[3,1,64,128]{3,2,1,0:T(8,128)S(1)}, u32[]{:S(2)}, u32[]{:S(2)}) %collective-permute-start.12) | collective-permute-done | bytes 98336 | tf_op jit(solution)/shard_map/ppermute | solution.py:16
  116.0 0.5 collective-permute-start.14
  116.5 1.0 fusion.161
  117.5 4.2 %collective-permute-done.14 = f32[3,18,1,128]{3,2,1,0:T(1,128)S(1)} collective-permute-done((f32[3,18,1,128]{3,2,1,0:T(1,128)S(1)}, f32[3,18,1,128]{3,2,1,0:T(1,128)S(1)}, u32[]{:S(2)}, u32[]{:S(2)}) %collective-permute-start.14) | collective-permute-done | bytes 27680 | tf_op jit(solution)/shard_map/ppermute | solution.py:16
  121.7 0.3 pad_maximum_fusion.7
  122.0 0.6 fusion.167
  122.7 0.4 maximum_maximum_fusion.3
  123.0 7.3 %fusion.4 = bf16[3,16,64,128]{3,2,1,0:T(8,128)(2,1)} fusion(f32[3,16,64,128]{3,2,1,0:T(8,128)S(1)} %fusion.38, f32[3,18,66,64]{3,2,1,0:T(8,128)S(1)} %get-tuple-element.3, f32[3,18,66,64]{3,2,1,0:T(8,128)S(1)} %get-tuple-element.2, f32[3,18,65,128]{3,2,1,0:T(8,128)S(1)} %get-tuple-element.11, f32[3,1,64,128]{3,2,1,0:T(8,128)S(1)} %collective-permute-done.13, ...), kind=kLoop, calls=%fused_computation.17 | loop fusion | flops 20054016 | bytes 24827904 | tf_op jit(solution)/shard_map/convert_element_type | solution.py:75
  130.3 3.2 %reshape.117 = bf16[3072,2,64]{2,1,0:T(2,128)(2,1)S(1)} reshape(bf16[3,16,64,128]{3,2,1,0:T(8,128)(2,1)} %fusion.4) | data formatting | bytes 1572864 | tf_op jit(solution)/shard_map/reshape | solution.py:77
  133.5 3.1 %fusion.171 = (bf16[3072,1,64]{2,1,0:T(2,128)(2,1)S(1)}, bf16[3072,1,64]{2,1,0:T(2,128)(2,1)}) fusion(bf16[3072,2,64]{2,1,0:T(2,128)(2,1)S(1)} %reshape.117), kind=kLoop, calls=%fused_computation.398 | loop fusion | bytes 1572864 | tf_op jit(solution)/shard_map/slice | solution.py:62
  136.6 3.5 %copy.16 = bf16[3072,1,64]{0,2,1:T(8,128)(2,1)S(1)} copy(bf16[3072,1,64]{2,1,0:T(2,128)(2,1)} %get-tuple-element.35) | data formatting | bytes 786432
  140.1 1.5 copy.18
  141.6 0.3 fusion.164
  141.9 0.2 fusion.137
  142.2 17.5 %all-gather = f32[1024,64]{1,0:T(8,128)S(1)} all-gather(f32[64,64]{1,0:T(8,128)S(1)} %copy.10), channel_id=2, replica_groups=mesh['gx'=16,'gz'=16] {'gz'}, dimensions={0}, use_global_device_ids=true | all-gather | bytes 278528 | tf_op jit(solution)/shard_map/all_gather | solution.py:79
  159.8 71.9 %all-reduce = f32[64,64]{1,0:T(8,128)S(1)} all-reduce(f32[64,64]{1,0:T(8,128)S(1)} %reduce_sum.9), channel_id=3, replica_groups=mesh['gx'=16,'gz'=16] {'gx'}, use_global_device_ids=true, to_apply=%region_1.2.clone | all-reduce | flops 4096 | bytes 32768
  231.7 0.6 constant_dynamic-slice_fusion
  (127 shorter events, 3.3 us)
Async XLA Ops:
  0.6 10.3 %copy-start.20 = (f32[36,16,64]{2,1,0:T(8,128)S(1)}, f32[36,16,64]{2,1,0:T(8,128)}, u32[]{:S(2)}) copy-start(f32[36,16,64]{2,1,0:T(8,128)} %param.6) | copy-start | bytes 442372
  2.2 10.1 %copy-start.21 = (f32[18,16,64]{2,1,0:T(8,128)S(1)}, f32[18,16,64]{2,1,0:T(8,128)}, u32[]{:S(2)}) copy-start(f32[18,16,64]{2,1,0:T(8,128)} %param.7) | copy-start | bytes 221188
  2.2 28.2 %collective-permute-start.1 = (f32[3,1,64,128]{3,2,1,0:T(8,128)}, f32[3,1,64,128]{3,2,1,0:T(8,128)S(1)}, u32[]{:S(2)}, u32[]{:S(2)}) collective-permute-start(f32[3,1,64,128]{3,2,1,0:T(8,128)} %get-tuple-element.45), channel_id=1, source_target_pairs={{16,0},{32,16},{48,32},{64,48},{80,64},{96,80},{112,96},{128,112},... | collective-permute-start | bytes 294920 | tf_op jit(solution)/shard_map/ppermute | solution.py:17
  9.6 20.8 %collective-permute-start = (f32[3,1,64,128]{3,2,1,0:T(8,128)}, f32[3,1,64,128]{3,2,1,0:T(8,128)S(1)}, u32[]{:S(2)}, u32[]{:S(2)}) collective-permute-start(f32[3,1,64,128]{3,2,1,0:T(8,128)} %get-tuple-element.44), channel_id=1, source_target_pairs={{0,16},{16,32},{32,48},{48,64},{64,80},{80,96},{96,112},{112,128},... | collective-permute-start | bytes 294920 | tf_op jit(solution)/shard_map/ppermute | solution.py:16
  15.6 3.6 %copy-start.33 = (f32[16,64]{1,0:T(8,128)S(1)}, f32[16,64]{1,0:T(8,128)}, u32[]{:S(2)}) copy-start(f32[16,64]{1,0:T(8,128)} %get-tuple-element.47) | copy-start | bytes 12292
  15.6 3.6 %copy-start.34 = (f32[16,64]{1,0:T(8,128)S(1)}, f32[16,64]{1,0:T(8,128)}, u32[]{:S(2)}) copy-start(f32[16,64]{1,0:T(8,128)} %get-tuple-element.48) | copy-start | bytes 12292
  15.6 3.6 %copy-start.35 = (f32[16,64]{1,0:T(8,128)S(1)}, f32[16,64]{1,0:T(8,128)}, u32[]{:S(2)}) copy-start(f32[16,64]{1,0:T(8,128)} %get-tuple-element.49) | copy-start | bytes 12292
  15.6 3.6 %copy-start.36 = (f32[16,64]{1,0:T(8,128)S(1)}, f32[16,64]{1,0:T(8,128)}, u32[]{:S(2)}) copy-start(f32[16,64]{1,0:T(8,128)} %get-tuple-element.50) | copy-start | bytes 12292
  15.6 3.6 %copy-start.37 = (f32[16,64]{1,0:T(8,128)S(1)}, f32[16,64]{1,0:T(8,128)}, u32[]{:S(2)}) copy-start(f32[16,64]{1,0:T(8,128)} %get-tuple-element.51) | copy-start | bytes 12292
  15.6 3.6 %copy-start.38 = (f32[16,64]{1,0:T(8,128)S(1)}, f32[16,64]{1,0:T(8,128)}, u32[]{:S(2)}) copy-start(f32[16,64]{1,0:T(8,128)} %get-tuple-element.52) | copy-start | bytes 12292
  15.6 3.6 %copy-start.39 = (f32[16,64]{1,0:T(8,128)S(1)}, f32[16,64]{1,0:T(8,128)}, u32[]{:S(2)}) copy-start(f32[16,64]{1,0:T(8,128)} %get-tuple-element.53) | copy-start | bytes 12292
  15.6 3.6 %copy-start.40 = (f32[16,64]{1,0:T(8,128)S(1)}, f32[16,64]{1,0:T(8,128)}, u32[]{:S(2)}) copy-start(f32[16,64]{1,0:T(8,128)} %get-tuple-element.54) | copy-start | bytes 12292
  15.6 3.6 %copy-start.41 = (f32[16,64]{1,0:T(8,128)S(1)}, f32[16,64]{1,0:T(8,128)}, u32[]{:S(2)}) copy-start(f32[16,64]{1,0:T(8,128)} %get-tuple-element.55) | copy-start | bytes 12292
  15.7 3.6 %copy-start.42 = (f32[16,64]{1,0:T(8,128)S(1)}, f32[16,64]{1,0:T(8,128)}, u32[]{:S(2)}) copy-start(f32[16,64]{1,0:T(8,128)} %get-tuple-element.56) | copy-start | bytes 12292
  15.7 3.6 %copy-start.43 = (f32[16,64]{1,0:T(8,128)S(1)}, f32[16,64]{1,0:T(8,128)}, u32[]{:S(2)}) copy-start(f32[16,64]{1,0:T(8,128)} %get-tuple-element.57) | copy-start | bytes 12292
  15.7 3.6 %copy-start.44 = (f32[16,64]{1,0:T(8,128)S(1)}, f32[16,64]{1,0:T(8,128)}, u32[]{:S(2)}) copy-start(f32[16,64]{1,0:T(8,128)} %get-tuple-element.58) | copy-start | bytes 12292
  15.7 3.6 %copy-start.45 = (f32[16,64]{1,0:T(8,128)S(1)}, f32[16,64]{1,0:T(8,128)}, u32[]{:S(2)}) copy-start(f32[16,64]{1,0:T(8,128)} %get-tuple-element.59) | copy-start | bytes 12292
  15.7 3.6 %copy-start.46 = (f32[16,64]{1,0:T(8,128)S(1)}, f32[16,64]{1,0:T(8,128)}, u32[]{:S(2)}) copy-start(f32[16,64]{1,0:T(8,128)} %get-tuple-element.60) | copy-start | bytes 12292
  15.7 3.6 %copy-start.47 = (f32[16,64]{1,0:T(8,128)S(1)}, f32[16,64]{1,0:T(8,128)}, u32[]{:S(2)}) copy-start(f32[16,64]{1,0:T(8,128)} %get-tuple-element.61) | copy-start | bytes 12292
  15.7 3.6 %copy-start.48 = (f32[16,64]{1,0:T(8,128)S(1)}, f32[16,64]{1,0:T(8,128)}, u32[]{:S(2)}) copy-start(f32[16,64]{1,0:T(8,128)} %get-tuple-element.62) | copy-start | bytes 12292
  15.7 3.6 %copy-start.49 = (f32[16,64]{1,0:T(8,128)S(1)}, f32[16,64]{1,0:T(8,128)}, u32[]{:S(2)}) copy-start(f32[16,64]{1,0:T(8,128)} %get-tuple-element.80) | copy-start | bytes 12292
  15.7 3.6 %copy-start.50 = (f32[16,64]{1,0:T(8,128)S(1)}, f32[16,64]{1,0:T(8,128)}, u32[]{:S(2)}) copy-start(f32[16,64]{1,0:T(8,128)} %get-tuple-element.81) | copy-start | bytes 12292
  19.4 4.0 %copy-start.22 = (f32[16,64]{1,0:T(8,128)S(1)}, f32[16,64]{1,0:T(8,128)}, u32[]{:S(2)}) copy-start(f32[16,64]{1,0:T(8,128)} %get-tuple-element.69) | copy-start | bytes 12292
  19.4 4.0 %copy-start.23 = (f32[16,64]{1,0:T(8,128)S(1)}, f32[16,64]{1,0:T(8,128)}, u32[]{:S(2)}) copy-start(f32[16,64]{1,0:T(8,128)} %get-tuple-element.70) | copy-start | bytes 12292
  19.4 4.0 %copy-start.24 = (f32[16,64]{1,0:T(8,128)S(1)}, f32[16,64]{1,0:T(8,128)}, u32[]{:S(2)}) copy-start(f32[16,64]{1,0:T(8,128)} %get-tuple-element.71) | copy-start | bytes 12292
  19.4 4.0 %copy-start.25 = (f32[16,64]{1,0:T(8,128)S(1)}, f32[16,64]{1,0:T(8,128)}, u32[]{:S(2)}) copy-start(f32[16,64]{1,0:T(8,128)} %get-tuple-element.72) | copy-start | bytes 12292
  19.4 4.0 %copy-start.26 = (f32[16,64]{1,0:T(8,128)S(1)}, f32[16,64]{1,0:T(8,128)}, u32[]{:S(2)}) copy-start(f32[16,64]{1,0:T(8,128)} %get-tuple-element.73) | copy-start | bytes 12292
  19.4 4.0 %copy-start.27 = (f32[16,64]{1,0:T(8,128)S(1)}, f32[16,64]{1,0:T(8,128)}, u32[]{:S(2)}) copy-start(f32[16,64]{1,0:T(8,128)} %get-tuple-element.74) | copy-start | bytes 12292
  19.4 4.0 %copy-start.28 = (f32[16,64]{1,0:T(8,128)S(1)}, f32[16,64]{1,0:T(8,128)}, u32[]{:S(2)}) copy-start(f32[16,64]{1,0:T(8,128)} %get-tuple-element.75) | copy-start | bytes 12292
  19.4 4.0 %copy-start.29 = (f32[16,64]{1,0:T(8,128)S(1)}, f32[16,64]{1,0:T(8,128)}, u32[]{:S(2)}) copy-start(f32[16,64]{1,0:T(8,128)} %get-tuple-element.76) | copy-start | bytes 12292
  19.4 4.0 %copy-start.30 = (f32[16,64]{1,0:T(8,128)S(1)}, f32[16,64]{1,0:T(8,128)}, u32[]{:S(2)}) copy-start(f32[16,64]{1,0:T(8,128)} %get-tuple-element.77) | copy-start | bytes 12292
  19.4 4.0 %copy-start.31 = (f32[16,64]{1,0:T(8,128)S(1)}, f32[16,64]{1,0:T(8,128)}, u32[]{:S(2)}) copy-start(f32[16,64]{1,0:T(8,128)} %get-tuple-element.78) | copy-start | bytes 12292
  19.5 4.0 %copy-start.32 = (f32[16,64]{1,0:T(8,128)S(1)}, f32[16,64]{1,0:T(8,128)}, u32[]{:S(2)}) copy-start(f32[16,64]{1,0:T(8,128)} %get-tuple-element.79) | copy-start | bytes 12292
  31.1 14.1 %collective-permute-start.3 = (f32[3,18,1,128]{3,2,1,0:T(1,128)}, f32[3,18,1,128]{3,2,1,0:T(1,128)S(1)}, u32[]{:S(2)}, u32[]{:S(2)}) collective-permute-start(f32[3,18,1,128]{3,2,1,0:T(1,128)} %get-tuple-element.25), channel_id=1, source_target_pairs={{1,0},{2,1},{3,2},{4,3},{5,4},{6,5},{7,6},{8,7},{9,8},{10,9},{11,1... | collective-permute-start | bytes 82952 | tf_op jit(solution)/shard_map/ppermute | solution.py:17
  34.1 11.1 %collective-permute-start.2 = (f32[3,18,1,128]{3,2,1,0:T(1,128)}, f32[3,18,1,128]{3,2,1,0:T(1,128)S(1)}, u32[]{:S(2)}, u32[]{:S(2)}) collective-permute-start(f32[3,18,1,128]{3,2,1,0:T(1,128)} %get-tuple-element.24), channel_id=1, source_target_pairs={{0,1},{1,2},{2,3},{3,4},{4,5},{5,6},{6,7},{7,8},{8,9},{9,10},{10,1... | collective-permute-start | bytes 82952 | tf_op jit(solution)/shard_map/ppermute | solution.py:16
  35.8 8.2 %copy-start.51 = (u32[256]{0:T(256)S(1)}, u32[256]{0:T(256)}, u32[]{:S(2)}) copy-start(u32[256]{0:T(256)} %constant.6) | copy-start | bytes 3076
  45.6 1.6 copy-start.15
  45.6 1.8 copy-start.16
  45.6 1.9 copy-start.17
  46.3 1.6 copy-start
  46.3 1.8 copy-start.1
  46.3 1.9 copy-start.2
  46.3 2.1 copy-start.3
  46.3 2.2 copy-start.4
  46.3 2.3 %copy-start.5 = (f32[16,64,128]{2,1,0:T(8,128)S(1)}, f32[16,64,128]{2,1,0:T(8,128)}, u32[]{:S(2)}) copy-start(f32[16,64,128]{2,1,0:T(8,128)} %get-tuple-element.117) | copy-start | bytes 1572868
  46.3 2.5 %copy-start.6 = (f32[16,64,128]{2,1,0:T(8,128)S(1)}, f32[16,64,128]{2,1,0:T(8,128)}, u32[]{:S(2)}) copy-start(f32[16,64,128]{2,1,0:T(8,128)} %get-tuple-element.100) | copy-start | bytes 1572868
  46.3 2.6 %copy-start.7 = (f32[16,64,128]{2,1,0:T(8,128)S(1)}, f32[16,64,128]{2,1,0:T(8,128)}, u32[]{:S(2)}) copy-start(f32[16,64,128]{2,1,0:T(8,128)} %get-tuple-element.101) | copy-start | bytes 1572868
  46.3 2.8 %copy-start.8 = (f32[16,64,128]{2,1,0:T(8,128)S(1)}, f32[16,64,128]{2,1,0:T(8,128)}, u32[]{:S(2)}) copy-start(f32[16,64,128]{2,1,0:T(8,128)} %get-tuple-element.102) | copy-start | bytes 1572868
  46.3 2.9 %copy-start.9 = (f32[16,64,128]{2,1,0:T(8,128)S(1)}, f32[16,64,128]{2,1,0:T(8,128)}, u32[]{:S(2)}) copy-start(f32[16,64,128]{2,1,0:T(8,128)} %get-tuple-element.103) | copy-start | bytes 1572868
  46.4 3.1 %copy-start.10 = (f32[16,64,128]{2,1,0:T(8,128)S(1)}, f32[16,64,128]{2,1,0:T(8,128)}, u32[]{:S(2)}) copy-start(f32[16,64,128]{2,1,0:T(8,128)} %get-tuple-element.104) | copy-start | bytes 1572868
  55.9 7.2 %collective-permute-start.5 = (f32[3,1,64,128]{3,2,1,0:T(8,128)S(1)}, f32[3,1,64,128]{3,2,1,0:T(8,128)S(1)}, u32[]{:S(2)}, u32[]{:S(2)}) collective-permute-start(f32[3,1,64,128]{3,2,1,0:T(8,128)S(1)} %get-tuple-element.43), channel_id=1, source_target_pairs={{16,0},{32,16},{48,32},{64,48},{80,64},{96,80},{112,96},{128,112},... | collective-permute-start | bytes 294920 | tf_op jit(solution)/shard_map/ppermute | solution.py:17
  60.9 8.2 %collective-permute-start.4 = (f32[3,1,64,128]{3,2,1,0:T(8,128)S(1)}, f32[3,1,64,128]{3,2,1,0:T(8,128)S(1)}, u32[]{:S(2)}, u32[]{:S(2)}) collective-permute-start(f32[3,1,64,128]{3,2,1,0:T(8,128)S(1)} %get-tuple-element.42), channel_id=1, source_target_pairs={{0,16},{16,32},{32,48},{48,64},{64,80},{80,96},{96,112},{112,128},... | collective-permute-start | bytes 294920 | tf_op jit(solution)/shard_map/ppermute | solution.py:16
  69.1 4.7 %collective-permute-start.7 = (f32[3,18,1,128]{3,2,1,0:T(1,128)S(1)}, f32[3,18,1,128]{3,2,1,0:T(1,128)S(1)}, u32[]{:S(2)}, u32[]{:S(2)}) collective-permute-start(f32[3,18,1,128]{3,2,1,0:T(1,128)S(1)} %get-tuple-element.21), channel_id=1, source_target_pairs={{1,0},{2,1},{3,2},{4,3},{5,4},{6,5},{7,6},{8,7},{9,8},{10,9},{11,1... | collective-permute-start | bytes 82952 | tf_op jit(solution)/shard_map/ppermute | solution.py:17
  72.2 5.4 %collective-permute-start.6 = (f32[3,18,1,128]{3,2,1,0:T(1,128)S(1)}, f32[3,18,1,128]{3,2,1,0:T(1,128)S(1)}, u32[]{:S(2)}, u32[]{:S(2)}) collective-permute-start(f32[3,18,1,128]{3,2,1,0:T(1,128)S(1)} %get-tuple-element.20), channel_id=1, source_target_pairs={{0,1},{1,2},{2,3},{3,4},{4,5},{5,6},{6,7},{7,8},{8,9},{9,10},{10,1... | collective-permute-start | bytes 82952 | tf_op jit(solution)/shard_map/ppermute | solution.py:16
  85.4 4.7 %collective-permute-start.9 = (f32[3,1,64,128]{3,2,1,0:T(8,128)S(1)}, f32[3,1,64,128]{3,2,1,0:T(8,128)S(1)}, u32[]{:S(2)}, u32[]{:S(2)}) collective-permute-start(f32[3,1,64,128]{3,2,1,0:T(8,128)S(1)} %get-tuple-element.41), channel_id=1, source_target_pairs={{16,0},{32,16},{48,32},{64,48},{80,64},{96,80},{112,96},{128,112},... | collective-permute-start | bytes 294920 | tf_op jit(solution)/shard_map/ppermute | solution.py:17
  85.5 8.3 %collective-permute-start.8 = (f32[3,1,64,128]{3,2,1,0:T(8,128)S(1)}, f32[3,1,64,128]{3,2,1,0:T(8,128)S(1)}, u32[]{:S(2)}, u32[]{:S(2)}) collective-permute-start(f32[3,1,64,128]{3,2,1,0:T(8,128)S(1)} %get-tuple-element.40), channel_id=1, source_target_pairs={{0,16},{16,32},{32,48},{48,64},{64,80},{80,96},{96,112},{112,128},... | collective-permute-start | bytes 294920 | tf_op jit(solution)/shard_map/ppermute | solution.py:16
  93.9 1.6 collective-permute-start.11
  94.0 5.7 %collective-permute-start.10 = (f32[3,18,1,128]{3,2,1,0:T(1,128)S(1)}, f32[3,18,1,128]{3,2,1,0:T(1,128)S(1)}, u32[]{:S(2)}, u32[]{:S(2)}) collective-permute-start(f32[3,18,1,128]{3,2,1,0:T(1,128)S(1)} %get-tuple-element.16), channel_id=1, source_target_pairs={{0,1},{1,2},{2,3},{3,4},{4,5},{5,6},{6,7},{7,8},{8,9},{9,10},{10,1... | collective-permute-start | bytes 82952 | tf_op jit(solution)/shard_map/ppermute | solution.py:16
  107.5 4.7 %collective-permute-start.13 = (f32[3,1,64,128]{3,2,1,0:T(8,128)S(1)}, f32[3,1,64,128]{3,2,1,0:T(8,128)S(1)}, u32[]{:S(2)}, u32[]{:S(2)}) collective-permute-start(f32[3,1,64,128]{3,2,1,0:T(8,128)S(1)} %get-tuple-element.39), channel_id=1, source_target_pairs={{16,0},{32,16},{48,32},{64,48},{80,64},{96,80},{112,96},{128,112},... | collective-permute-start | bytes 294920 | tf_op jit(solution)/shard_map/ppermute | solution.py:17
  107.6 8.3 %collective-permute-start.12 = (f32[3,1,64,128]{3,2,1,0:T(8,128)S(1)}, f32[3,1,64,128]{3,2,1,0:T(8,128)S(1)}, u32[]{:S(2)}, u32[]{:S(2)}) collective-permute-start(f32[3,1,64,128]{3,2,1,0:T(8,128)S(1)} %get-tuple-element.38), channel_id=1, source_target_pairs={{0,16},{16,32},{32,48},{48,64},{64,80},{80,96},{96,112},{112,128},... | collective-permute-start | bytes 294920 | tf_op jit(solution)/shard_map/ppermute | solution.py:16
  115.9 1.6 collective-permute-start.15
  116.0 5.7 %collective-permute-start.14 = (f32[3,18,1,128]{3,2,1,0:T(1,128)S(1)}, f32[3,18,1,128]{3,2,1,0:T(1,128)S(1)}, u32[]{:S(2)}, u32[]{:S(2)}) collective-permute-start(f32[3,18,1,128]{3,2,1,0:T(1,128)S(1)} %get-tuple-element.12), channel_id=1, source_target_pairs={{0,1},{1,2},{2,3},{3,4},{4,5},{5,6},{6,7},{7,8},{8,9},{9,10},{10,1... | collective-permute-start | bytes 82952 | tf_op jit(solution)/shard_map/ppermute | solution.py:16
  136.6 5.1 %copy-start.18 = (bf16[3072,1,64]{0,2,1:T(8,128)(2,1)S(1)}, bf16[3072,1,64]{0,2,1:T(8,128)(2,1)}, u32[]{:S(2)}) copy-start(bf16[3072,1,64]{0,2,1:T(8,128)(2,1)} %copy.17) | copy-start | bytes 1179652
  140.1 1.8 copy-start.19
  (4 other events, 5.2 us)
